TPU v7x, 32 devices: a whole 2x2x4 slice. The times are simulated.
32 devices in a mesh: src: 8 (over z, core), tgt: 4 (over y, x).
Axes of the slice: x: 2, y: 2, z: 4, core: 2. Of those that a mesh axis runs over, the one named last changes fastest.
Arguments:
- charges: bfloat16 [65536, 64], P(('src', 'tgt')), may hold values from -6 to 6
- near_tiles: bfloat16 [4096, 128, 128], P(('src', 'tgt')), may hold values from -0.0625 to 0.0625
- near_tgt: int32 [4096], P(('src', 'tgt')), may hold values from 0 to 127
- near_src: int32 [4096], P(('src', 'tgt')), may hold values from 0 to 15
- leaf_basis: bfloat16 [512, 64, 128], P(('src', 'tgt')), may hold values from -0.125 to 0.125
- transfer: float32 [8, 3, 64, 128], P('src'), may hold values from -0.5 to 0.5
- coupling: bfloat16 [8, 512, 64, 256], P('src', 'tgt'), may hold values from -0.375 to 0.375
- far_node: int32 [8, 512, 4], P('src', 'tgt'), may hold values from 0 to 6
- target_basis: bfloat16 [512, 64, 128], P('tgt'), may hold values from -0.25 to 0.25
Outputs:
- potential: bfloat16 [65536, 64], P('tgt')
All inputs are finite; a program needn't handle non-finite values.
Results may differ from a plain program's by a relative error of at most 0.0057.
Values may be sent and summed in bfloat16 or wider, within the bound.
No kernel may reach another device: no remote copies, remote signals or barrier semaphores. Data moves between devices by JAX's collectives and lax.ppermute only.
A program may use at most 128 MiB of HBM per device.

v0:
```python
import jax
import jax.numpy as jnp
from jax import lax
from jax.sharding import PartitionSpec as P


def climb(edges, leaves):
    levels = [leaves]
    level = leaves
    width = leaves.shape[0]
    while width > 1:
        width = width // 2
        edge_slab = edges[width - 1 : 2 * width - 1]
        pairs = level.reshape(width, 2 * level.shape[1], level.shape[2])
        level = jnp.einsum("prc,pcn->prn", edge_slab, pairs, precision=lax.Precision.HIGHEST)
        levels.insert(0, level)
    return jnp.concatenate(levels, axis=0)


def shards(
    charges, near_tiles, near_tgt, near_src, leaf_basis, transfer, coupling, far_node, target_basis
):
    groups = lax.axis_size("tgt")
    tile = near_tiles.shape[1]
    slots = near_tiles.shape[0] // groups
    nrhs = charges.shape[1]
    tdev = leaf_basis.shape[0]
    tgt_tiles = target_basis.shape[0]
    local_leaves = charges.reshape(tdev, tile, nrhs)
    block_x = lax.all_gather(charges, "tgt", axis=0, tiled=True)
    block_leaves = block_x.reshape(groups * tdev, tile, nrhs)
    got_tiles, got_tgt, got_src = (
        lax.all_to_all(
            near_tiles.reshape(groups, slots, tile, tile),
            "tgt",
            split_axis=0,
            concat_axis=0,
            tiled=True,
        ),
        lax.all_to_all(
            near_tgt.reshape(groups, slots), "tgt", split_axis=0, concat_axis=0, tiled=True
        ),
        lax.all_to_all(
            near_src.reshape(groups, slots), "tgt", split_axis=0, concat_axis=0, tiled=True
        ),
    )
    sender = jnp.arange(groups, dtype=jnp.int32)[:, None] * tdev
    picked = block_leaves[(got_src + sender).reshape(-1)]
    products = jnp.einsum(
        "kab,kbn->kan",
        got_tiles.reshape(groups * slots, tile, tile),
        picked,
        preferred_element_type=jnp.float32,
    ).astype(jnp.bfloat16)
    results = products.reshape(groups * slots, tile * nrhs)
    onehot = (
        got_tgt.reshape(-1)[None, :] == jnp.arange(tgt_tiles, dtype=jnp.int32)[:, None]
    ).astype(jnp.bfloat16)
    near_part = jnp.dot(onehot, results, preferred_element_type=jnp.float32).reshape(
        tgt_tiles, tile, nrhs
    )
    own_root = jnp.einsum(
        "irp,ipn->rn", leaf_basis, local_leaves, preferred_element_type=jnp.float32
    )
    roots = lax.all_gather(own_root[None], "tgt", axis=0, tiled=True)
    table_b = climb(transfer[0], roots).astype(jnp.bfloat16)
    chosen = table_b[far_node[0]]
    stacked = chosen.reshape(chosen.shape[0], chosen.shape[1] * chosen.shape[2], chosen.shape[3])
    zed = jnp.einsum(
        "trc,tcn->trn", coupling[0], stacked, preferred_element_type=jnp.float32
    ).astype(jnp.bfloat16)
    far_part = jnp.einsum("trp,trn->tpn", target_basis, zed, preferred_element_type=jnp.float32)
    total = lax.psum(near_part + far_part, "src")
    return total.reshape(tgt_tiles * tile, nrhs).astype(jnp.bfloat16)


def solution(mesh):
    in_specs = (
        P(("src", "tgt"), None),
        P(("src", "tgt"), None, None),
        P(("src", "tgt")),
        P(("src", "tgt")),
        P(("src", "tgt"), None, None),
        P("src", None, None, None),
        P("src", "tgt", None, None),
        P("src", "tgt", None),
        P("tgt", None, None),
    )
    out_specs = P("tgt", None)
    return jax.shard_map(shards, mesh=mesh, in_specs=in_specs, out_specs=out_specs, check_vma=False)
```

profile of v0, /device:TPU:0, one launch (start us, length us, event | category | flops | bytes accessed | tf_op | source)
XLA Modules:
  0.0 229.9 jit_solution(22342178664808645)
XLA Ops:
  6.5 1.5 all_to_all.19
  8.0 5.2 %all-to-all-start.1 = ((s32[4,1,32]{2,1,0:T(1,128)}), s32[4,1,32]{2,1,0:T(1,128)S(1)}, u32[]{:S(2)}, u32[]{:S(2)}) async-start(s32[4,1,32]{2,1,0:T(1,128)} %bitcast.2), calls=%async_computation.1 | async-start | bytes 4096 | tf_op jit(solution)/shard_map/all_to_all | solution.py:43
  13.2 0.7 all_to_all.17
  13.9 3.8 %all-to-all-done.1 = s32[4,1,32]{2,1,0:T(1,128)S(1)} async-done(((s32[4,1,32]{2,1,0:T(1,128)}), s32[4,1,32]{2,1,0:T(1,128)S(1)}, u32[]{:S(2)}, u32[]{:S(2)}) %all-to-all-start.1) | async-done | bytes 544 | tf_op jit(solution)/shard_map/all_to_all | solution.py:43
  17.7 7.0 %all_to_all.26 = s32[4,1,32]{2,1,0:T(1,128)S(1)} all-to-all(s32[4,1,32]{2,1,0:T(1,128)S(1)} %bitcast.80), channel_id=1, replica_groups=mesh['src'=8,'tgt'=4] {'tgt'}, dimensions={0} | all-to-all | bytes 1024 | tf_op jit(solution)/shard_map/all_to_all | solution.py:40
  24.7 5.1 %all-to-all-start.2 = ((bf16[4,32,128,128]{3,2,1,0:T(8,128)(2,1)}), bf16[4,32,128,128]{3,2,1,0:T(8,128)(2,1)}, u32[]{:S(2)}, u32[]{:S(2)}) async-start(bf16[4,32,128,128]{3,2,1,0:T(8,128)(2,1)} %bitcast.77), calls=%async_computation.2 | async-start | bytes 8388608 | tf_op jit(solution)/shard_map/all_to_all | solution.py:33
  29.8 0.7 all-gather.3.cloned.1.call-update
  30.5 0.2 convolution_bitcast_fusion.1
  30.8 56.5 %all-gather = f32[256,64]{1,0:T(8,128)S(1)} all-gather(f32[64,64]{1,0:T(8,128)S(1)} %convolution_bitcast_fusion.1), channel_id=2, replica_groups=mesh['src'=8,'tgt'=4] {'tgt'}, dimensions={0}, use_global_device_ids=true | all-gather | bytes 81920 | tf_op jit(solution)/shard_map/all_gather | solution.py:65
  87.3 0.4 fusion.20
  87.9 0.2 fusion.9
  88.3 0.1 copy.67
  88.4 0.1 reshape.129
  88.7 13.5 %gather_fusion.1 = bf16[512,64,64]{2,1,0:T(8,128)(2,1)} fusion(bf16[7,64,64]{2,1,0:T(8,128)(2,1)S(1)} %pad_maximum_fusion, s32[1024]{0:T(1024)S(1)} %pad_clamp_fusion), kind=kCustom, calls=%fused_computation.1 | custom fusion | bytes 8390656 | tf_op jit(solution)/shard_map/gather | solution.py:67
  102.2 10.1 %fusion.3 = f32[128,64,128]{2,1,0:T(8,128)} fusion(bf16[128,64,128]{2,1,0:T(8,128)(2,1)S(1)} %copy-done, bf16[128,256,64]{2,1,0:T(8,128)(2,1)} %bitcast.75, bf16[1,128,64,256]{3,2,1,0:T(8,128)(2,1)} %param.15), kind=kOutput, calls=%fused_computation.7 | convolution fusion | flops 403177472 | bytes 14680064 | tf_op jit(solution)/shard_map/trp,trn->tpn/dot_general | solution.py:72
  112.2 0.5 broadcast.53
  112.8 0.7 reduce.6
  113.5 0.7 reduce.7
  114.3 1.5 copy_bitcast_fusion.1
  115.8 2.1 gather_fusion
  118.0 5.9 %convert_bitcast_fusion = bf16[128,64,128]{0,1,2:T(8,128)(2,1)S(1)} fusion(bf16[128,128,64]{1,2,0:T(8,128)(2,1)} %gather_fusion, bf16[128,128,128]{2,1,0:T(8,128)(2,1)} %bitcast.5), kind=kOutput, calls=%fused_computation.9 | convolution fusion | flops 269484032 | bytes 8388608 | tf_op jit(solution)/shard_map/kab,kbn->kan/dot_general | solution.py:49
  123.9 5.8 %bitcast_add_fusion = f32[128,128,64]{1,0,2:T(8,128)} fusion(f32[128,64,128]{2,1,0:T(8,128)S(1)} %copy-done.1, bf16[128,64,128]{0,1,2:T(8,128)(2,1)S(1)} %convert_bitcast_fusion, s32[128]{0:T(128)S(1)} %eq.15), kind=kOutput, calls=%fused_computation.2 | convolution fusion | flops 269500416 | bytes 10486272 | tf_op jit(solution)/shard_map/dot_general | solution.py:59
  129.7 89.2 %all-reduce.1 = bf16[128,128,64]{1,0,2:T(8,128)(2,1)} all-reduce(f32[128,128,64]{1,0,2:T(8,128)} %bitcast_add_fusion), channel_id=1, replica_groups=mesh['src'=8,'tgt'=4] {'src'}, use_global_device_ids=true, to_apply=%region_0.0 | all-reduce | flops 1048576 | bytes 6291456 | tf_op jit(solution)/shard_map/psum | solution.py:73
  218.8 4.3 %copy.87 = bf16[8,8,128,128]{3,1,2,0:T(8,128)(2,1)} copy(bf16[8,8,128,128]{3,2,1,0:T(8,128)(2,1)} %bitcast.76) | data formatting | bytes 4194304
  (30 shorter events, 0.8 us)
Async XLA Ops:
  6.5 95.6 %copy-start = (bf16[128,64,128]{2,1,0:T(8,128)(2,1)S(1)}, bf16[128,64,128]{2,1,0:T(8,128)(2,1)}, u32[]{:S(2)}) copy-start(bf16[128,64,128]{2,1,0:T(8,128)(2,1)} %param.17) | copy-start | bytes 6291460
  8.0 9.7 %all-to-all-start.1 = ((s32[4,1,32]{2,1,0:T(1,128)}), s32[4,1,32]{2,1,0:T(1,128)S(1)}, u32[]{:S(2)}, u32[]{:S(2)}) async-start(s32[4,1,32]{2,1,0:T(1,128)} %bitcast.2), calls=%async_computation.1 | async-start | bytes 4096 | tf_op jit(solution)/shard_map/all_to_all | solution.py:43
  24.7 5.8 %copy-start.2 = (bf16[2048,64]{0,1:T(8,128)(2,1)S(1)}, bf16[2048,64]{0,1:T(8,128)(2,1)}, u32[]{:S(2)}) copy-start(bf16[2048,64]{0,1:T(8,128)(2,1)} %param.9) | copy-start | bytes 786436
  24.7 5.8 %copy-start.3 = (bf16[16,64,128]{2,1,0:T(8,128)(2,1)S(1)}, bf16[16,64,128]{2,1,0:T(8,128)(2,1)}, u32[]{:S(2)}) copy-start(bf16[16,64,128]{2,1,0:T(8,128)(2,1)} %param.13) | copy-start | bytes 786436
  24.7 62.6 %copy-start.4 = (f32[1,3,64,128]{3,2,1,0:T(8,128)S(1)}, f32[1,3,64,128]{3,2,1,0:T(8,128)}, u32[]{:S(2)}) copy-start(f32[1,3,64,128]{3,2,1,0:T(8,128)} %param.14) | copy-start | bytes 294916
  24.7 63.1 %copy-start.5 = (s32[1,128,4]{1,2,0:T(4,128)S(1)}, s32[1,128,4]{1,2,0:T(4,128)}, u32[]{:S(2)}) copy-start(s32[1,128,4]{1,2,0:T(4,128)} %param.16) | copy-start | bytes 6148
  24.7 93.2 %all-to-all-start.2 = ((bf16[4,32,128,128]{3,2,1,0:T(8,128)(2,1)}), bf16[4,32,128,128]{3,2,1,0:T(8,128)(2,1)}, u32[]{:S(2)}, u32[]{:S(2)}) async-start(bf16[4,32,128,128]{3,2,1,0:T(8,128)(2,1)} %bitcast.77), calls=%async_computation.2 | async-start | bytes 8388608 | tf_op jit(solution)/shard_map/all_to_all | solution.py:33
  29.8 84.5 %all-gather.3.cloned.1.call-start = ((), (), s32[]{:S(2)}) async-start(), calls=%async_computation.3 | async-start | bytes 1310720 | tf_op jit(solution)/shard_map/all_gather | solution.py:30
  118.0 5.9 %copy-start.1 = (f32[128,64,128]{2,1,0:T(8,128)S(1)}, f32[128,64,128]{2,1,0:T(8,128)}, u32[]{:S(2)}) copy-start(f32[128,64,128]{2,1,0:T(8,128)} %fusion.3) | copy-start | bytes 12582916
Sparse Core Ops, SparseCore 0:
  32.5 44.3 all-gather.2
where the time goes:
time: 230 us
  blocking collectives  153 us (67%)
  local copies, waits for them, and re-layouts  25 us (11%)
  matrix products  22.5 us (10%)
  between operations  13.6 us (6%)
  starting transfers between devices  10.3 us (4%)
  waiting for transfers between devices  4.54 us (2%)
    psum x1, blocking collectives, shards(): total = lax.psum(near_part + far_part, 'src')  89.2 us
    all_gather x1, blocking collectives, shards(): roots = lax.all_gather(own_root[None], 'tgt', axis=0, tiled=True)  56.5 us
    gather x1, local copies, waits for them, and re-layouts, shards(): chosen = table_b[far_node[0]]  13.5 us
    dot_general x1, matrix products, shards(): jnp.einsum('trp,trn->tpn', target_basis, zed, preferred_element_type=jnp....  10.1 us
    all_to_all x1, blocking collectives, shards(): lax.all_to_all(near_tgt.reshape(groups, slots), 'tgt', split_axis=0, conc...  6.97 us
    dot_general x1, matrix products, shards(): jnp.einsum('kab,kbn->kan', got_tiles.reshape(groups * slots, tile, tile),...  5.94 us
    dot_general x1, matrix products, shards(): jnp.dot(onehot, results, preferred_element_type=jnp.float32)  5.76 us
    all_to_all x1, starting transfers between devices, shards(): lax.all_to_all(near_src.reshape(groups, slots), 'tgt', split_axis=0, conc...  5.16 us
  transfers between devices with their start and end apart: 3, of which 1 were waited for; matrix products, arithmetic and copies ran while one was open for 13% of the time, Pallas kernels for 0%

commit v1 on v0

--- a/solution.py
+++ b/solution.py
@@ -70,7 +70,7 @@
         "trc,tcn->trn", coupling[0], stacked, preferred_element_type=jnp.float32
     ).astype(jnp.bfloat16)
     far_part = jnp.einsum("trp,trn->tpn", target_basis, zed, preferred_element_type=jnp.float32)
-    total = lax.psum(near_part + far_part, "src")
+    total = lax.all_gather(near_part + far_part, axis_name="src").sum(axis=0)
     return total.reshape(tgt_tiles * tile, nrhs).astype(jnp.bfloat16)
 
 

time: 230 us -> 444 us (1.93)
  waiting for transfers between devices: 4.54 us -> 294 us
  blocking collectives: 153 us -> 63.5 us
  other arithmetic: 1.39 us -> 15.2 us
    all_gather x0 -> x1, waiting for transfers between devices: none -> 289 us  [shards(): total = lax.all_gather(near_part + far_part, axis_name='src').sum(axis=0)]
    psum x1 -> x0, blocking collectives: 89.2 us -> none  [shards(): total = lax.psum(near_part + far_part, 'src')]
    reduce_sum x0 -> x1, other arithmetic: none -> 13.9 us  [shards(): total = lax.all_gather(near_part + far_part, axis_name='src').sum(axis=0)]
  transfers between devices with their start and end apart: 3 -> 4, of which waited for: 1 -> 2; matrix products, arithmetic and copies ran while one was open for 13% -> 7% of each run, Pallas kernels for 0% -> 0%
where the time goes in v1:
time: 444 us
  waiting for transfers between devices  294 us (66%)
  blocking collectives  63.5 us (14%)
  local copies, waits for them, and re-layouts  25 us (6%)
  matrix products  22.7 us (5%)
  other arithmetic  15.2 us (3%)
  between operations  13.6 us (3%)
  starting transfers between devices  10.3 us (2%)
    all_gather x1, waiting for transfers between devices, shards(): total = lax.all_gather(near_part + far_part, axis_name='src').sum(axis=0)  289 us
    all_gather x1, blocking collectives, shards(): roots = lax.all_gather(own_root[None], 'tgt', axis=0, tiled=True)  56.5 us
    reduce_sum x1, other arithmetic, shards(): total = lax.all_gather(near_part + far_part, axis_name='src').sum(axis=0)  13.9 us
    gather x1, local copies, waits for them, and re-layouts, shards(): chosen = table_b[far_node[0]]  13.5 us
    dot_general x1, matrix products, shards(): jnp.einsum('trp,trn->tpn', target_basis, zed, preferred_element_type=jnp....  10.1 us
  transfers between devices with their start and end apart: 4, of which 2 were waited for; matrix products, arithmetic and copies ran while one was open for 7% of the time, Pallas kernels for 0%

profile of v1, /device:TPU:0, one launch (start us, length us, event | category | flops | bytes accessed | tf_op | source)
XLA Modules:
  0.0 443.9 jit_solution(10196314517709401212)
XLA Ops:
  6.5 1.5 all_to_all.19
  8.0 5.2 %all-to-all-start.1 = ((s32[4,1,32]{2,1,0:T(1,128)}), s32[4,1,32]{2,1,0:T(1,128)S(1)}, u32[]{:S(2)}, u32[]{:S(2)}) async-start(s32[4,1,32]{2,1,0:T(1,128)} %bitcast.2), calls=%async_computation.1 | async-start | bytes 4096 | tf_op jit(solution)/shard_map/all_to_all | solution.py:43
  13.2 0.7 all_to_all.17
  13.9 3.8 all-to-all-done.1
  17.7 7.0 %all_to_all.26 = s32[4,1,32]{2,1,0:T(1,128)S(1)} all-to-all(s32[4,1,32]{2,1,0:T(1,128)S(1)} %bitcast.82), channel_id=1, replica_groups=mesh['src'=8,'tgt'=4] {'tgt'}, dimensions={0} | all-to-all | bytes 1024 | tf_op jit(solution)/shard_map/all_to_all | solution.py:40
  24.7 5.1 %all-to-all-start.2 = ((bf16[4,32,128,128]{3,2,1,0:T(8,128)(2,1)}), bf16[4,32,128,128]{3,2,1,0:T(8,128)(2,1)}, u32[]{:S(2)}, u32[]{:S(2)}) async-start(bf16[4,32,128,128]{3,2,1,0:T(8,128)(2,1)} %bitcast.79), calls=%async_computation.2 | async-start | bytes 8388608 | tf_op jit(solution)/shard_map/all_to_all | solution.py:33
  29.8 0.7 all-gather.5.cloned.1.call-update
  30.6 0.2 convolution_bitcast_fusion.1
  30.8 56.5 %all-gather = f32[256,64]{1,0:T(8,128)S(1)} all-gather(f32[64,64]{1,0:T(8,128)S(1)} %convolution_bitcast_fusion.1), channel_id=2, replica_groups=mesh['src'=8,'tgt'=4] {'tgt'}, dimensions={0}, use_global_device_ids=true | all-gather | bytes 81920 | tf_op jit(solution)/shard_map/all_gather | solution.py:65
  87.4 0.4 fusion.20
  87.9 0.1 copy.67
  88.4 0.2 fusion.9
  88.7 13.5 %gather_fusion.1 = bf16[512,64,64]{2,1,0:T(8,128)(2,1)} fusion(bf16[7,64,64]{2,1,0:T(8,128)(2,1)S(1)} %pad_maximum_fusion, s32[1024]{0:T(1024)S(1)} %pad_clamp_fusion), kind=kCustom, calls=%fused_computation.1 | custom fusion | bytes 8390656 | tf_op jit(solution)/shard_map/gather | solution.py:67
  102.2 10.1 %fusion.3 = f32[128,64,128]{2,1,0:T(8,128)} fusion(bf16[128,64,128]{2,1,0:T(8,128)(2,1)S(1)} %copy-done, bf16[128,256,64]{2,1,0:T(8,128)(2,1)} %bitcast.77, bf16[1,128,64,256]{3,2,1,0:T(8,128)(2,1)} %param.15), kind=kOutput, calls=%fused_computation.7 | convolution fusion | flops 403177472 | bytes 14680064 | tf_op jit(solution)/shard_map/trp,trn->tpn/dot_general | solution.py:72
  112.3 0.5 broadcast.53
  112.8 0.7 reduce.6
  113.5 0.7 reduce.7
  114.3 1.5 copy_bitcast_fusion.1
  115.8 2.1 gather_fusion
  118.0 5.9 %convert_bitcast_fusion = bf16[128,64,128]{0,1,2:T(8,128)(2,1)S(1)} fusion(bf16[128,128,64]{1,2,0:T(8,128)(2,1)} %gather_fusion, bf16[128,128,128]{2,1,0:T(8,128)(2,1)} %bitcast.5), kind=kOutput, calls=%fused_computation.9 | convolution fusion | flops 269484032 | bytes 8388608 | tf_op jit(solution)/shard_map/kab,kbn->kan/dot_general | solution.py:49
  123.9 5.9 %bitcast_add_fusion = f32[128,128,64]{1,0,2:T(8,128)} fusion(f32[128,64,128]{2,1,0:T(8,128)S(1)} %copy-done.2, bf16[128,64,128]{0,1,2:T(8,128)(2,1)S(1)} %convert_bitcast_fusion, s32[128]{0:T(128)S(1)} %eq.15), kind=kOutput, calls=%fused_computation.2 | convolution fusion | flops 269500416 | bytes 10486272 | tf_op jit(solution)/shard_map/dot_general | solution.py:59
  129.8 289.0 %all-gather.7.cloned.1.call-done = f32[1024,128,64]{1,0,2:T(8,128)} async-done(((f32[128,128,64]{1,0,2:T(8,128)}), f32[1024,128,64]{1,0,2:T(8,128)}) %all-gather.7.cloned.1.call-update) | async-done | bytes 33554448 | tf_op jit(solution)/shard_map/all_gather | solution.py:73
  418.9 13.9 %reduce_sum.9 = bf16[128,128,64]{1,0,2:T(8,128)(2,1)} reduce(f32[8,128,128,64]{2,1,0,3:T(8,128)} %bitcast.76, f32[]{:T(128)} %constant.3.clone.1), dimensions={0}, to_apply=%region_0.0 | reduce | flops 7340032 | bytes 35651588 | tf_op jit(solution)/shard_map/reduce_sum | solution.py:73
  432.7 4.3 copy.87
  (35 shorter events, 1.0 us)
Async XLA Ops:
  6.5 95.7 %copy-start = (bf16[128,64,128]{2,1,0:T(8,128)(2,1)S(1)}, bf16[128,64,128]{2,1,0:T(8,128)(2,1)}, u32[]{:S(2)}) copy-start(bf16[128,64,128]{2,1,0:T(8,128)(2,1)} %param.17) | copy-start | bytes 6291460
  8.0 9.7 %all-to-all-start.1 = ((s32[4,1,32]{2,1,0:T(1,128)}), s32[4,1,32]{2,1,0:T(1,128)S(1)}, u32[]{:S(2)}, u32[]{:S(2)}) async-start(s32[4,1,32]{2,1,0:T(1,128)} %bitcast.2), calls=%async_computation.1 | async-start | bytes 4096 | tf_op jit(solution)/shard_map/all_to_all | solution.py:43
  24.7 5.9 %copy-start.3 = (bf16[2048,64]{0,1:T(8,128)(2,1)S(1)}, bf16[2048,64]{0,1:T(8,128)(2,1)}, u32[]{:S(2)}) copy-start(bf16[2048,64]{0,1:T(8,128)(2,1)} %param.9) | copy-start | bytes 786436
  24.7 5.9 %copy-start.4 = (bf16[16,64,128]{2,1,0:T(8,128)(2,1)S(1)}, bf16[16,64,128]{2,1,0:T(8,128)(2,1)}, u32[]{:S(2)}) copy-start(bf16[16,64,128]{2,1,0:T(8,128)(2,1)} %param.13) | copy-start | bytes 786436
  24.7 62.6 %copy-start.6 = (s32[1,128,4]{1,2,0:T(4,128)S(1)}, s32[1,128,4]{1,2,0:T(4,128)}, u32[]{:S(2)}) copy-start(s32[1,128,4]{1,2,0:T(4,128)} %param.16) | copy-start | bytes 6148
  24.7 62.6 %copy-start.5 = (f32[1,3,64,128]{3,2,1,0:T(8,128)S(1)}, f32[1,3,64,128]{3,2,1,0:T(8,128)}, u32[]{:S(2)}) copy-start(f32[1,3,64,128]{3,2,1,0:T(8,128)} %param.14) | copy-start | bytes 294916
  24.7 93.2 %all-to-all-start.2 = ((bf16[4,32,128,128]{3,2,1,0:T(8,128)(2,1)}), bf16[4,32,128,128]{3,2,1,0:T(8,128)(2,1)}, u32[]{:S(2)}, u32[]{:S(2)}) async-start(bf16[4,32,128,128]{3,2,1,0:T(8,128)(2,1)} %bitcast.79), calls=%async_computation.2 | async-start | bytes 8388608 | tf_op jit(solution)/shard_map/all_to_all | solution.py:33
  29.8 84.5 %all-gather.5.cloned.1.call-start = ((), (), s32[]{:S(2)}) async-start(), calls=%async_computation.3 | async-start | bytes 1310720 | tf_op jit(solution)/shard_map/all_gather | solution.py:30
  30.5 388.3 %all-gather.7.cloned.1.call-start = ((), (), s32[]{:S(2)}) async-start(), calls=%async_computation.4 | async-start | bytes 37748736 | tf_op jit(solution)/shard_map/all_gather | solution.py:73
  118.0 5.9 %copy-start.2 = (f32[128,64,128]{2,1,0:T(8,128)S(1)}, f32[128,64,128]{2,1,0:T(8,128)}, u32[]{:S(2)}) copy-start(f32[128,64,128]{2,1,0:T(8,128)} %fusion.3) | copy-start | bytes 12582916
  418.9 18.1 %copy-start.1 = (bf16[128,64,128]{2,1,0:T(8,128)(2,1)S(1)}, bf16[128,64,128]{2,1,0:T(8,128)(2,1)}, u32[]{:S(2)}) copy-start(bf16[128,64,128]{2,1,0:T(8,128)(2,1)} %param.17) | copy-start | bytes 6291460
Sparse Core Ops, SparseCore 0:
  32.5 44.3 all-gather.4
  130.0 288.8 all-gather.6
